TPU v7x, 512 devices: a whole 4x4x16 slice. The times are simulated.
512 devices in a mesh: row: 32 (over x, z_hi, core), col: 16 (over y, z_lo).
Axes of the slice: x: 4, y: 4, z: 16 (z_hi: 4, z_lo: 4; z = z_hi * 4 + z_lo), core: 2. Of those that a mesh axis runs over, the one named last changes fastest.
Arguments:
- pair: bfloat16 [512, 512, 128], P('row', 'col'), may hold values from -6 to 6
- targets: int32 [512, 512], P('row', 'col'), may hold values from 0 to 63, as said below
- w_gate: bfloat16 [128, 512], replicated, may hold values from -0.5 to 0.5
- w_up: bfloat16 [128, 512], replicated, may hold values from -0.5 to 0.5
- w_out: bfloat16 [512, 128], replicated, may hold values from -0.25 to 0.25
- w_head: bfloat16 [128, 64], replicated, may hold values from -16 to 16
Outputs:
- d_pair: bfloat16 [512, 512, 128], P('row', 'col')
- grad_gate: float32 [128, 512], P('row', 'col')
- grad_up: float32 [128, 512], P('row', 'col')
- grad_out: float32 [512, 128], P('row', 'col')
- grad_head: float32 [128, 64], P('row', 'col')
Inputs may be any that keep to these rules, and one draw needn't show every extreme that they name: symmetric: targets[i, j] equals targets[j, i].
All inputs are finite; a program needn't handle non-finite values.
Results may differ from a plain program's by a relative error of at most 0.015.
Values may be sent and summed in bfloat16 or wider, within the bound.
A program may use at most 64 MiB of HBM per device.

v0:
```python
import jax
import jax.numpy as jnp
from jax import lax
from jax.sharding import PartitionSpec as P

eps = 1e-05


def normalize(flat):
    values = flat.astype(jnp.float32)
    centre = values - jnp.mean(values, axis=-1, keepdims=True)
    scale_inv = lax.rsqrt(jnp.mean(centre * centre, axis=-1, keepdims=True) + eps)
    return (centre * scale_inv, scale_inv)


def forward_block(flat, w_gate, w_up, w_out, w_head):
    normed, scale_inv = normalize(flat)
    inputs = normed.astype(jnp.bfloat16)
    gate = jnp.dot(inputs, w_gate, preferred_element_type=jnp.float32)
    upper = jnp.dot(inputs, w_up, preferred_element_type=jnp.float32)
    hidden = (jax.nn.silu(gate) * upper).astype(jnp.bfloat16)
    updated = (
        flat.astype(jnp.float32) + jnp.dot(hidden, w_out, preferred_element_type=jnp.float32)
    ).astype(jnp.bfloat16)
    logits = jnp.dot(updated, w_head, preferred_element_type=jnp.float32).astype(jnp.bfloat16)
    return (updated, logits)


def backward_block(flat, updated, cotangent, w_gate, w_up, w_out, w_head):
    normed, scale_inv = normalize(flat)
    inputs = normed.astype(jnp.bfloat16)
    gate = jnp.dot(inputs, w_gate, preferred_element_type=jnp.float32)
    upper = jnp.dot(inputs, w_up, preferred_element_type=jnp.float32)
    sigma = jax.nn.sigmoid(gate)
    swish = jax.nn.silu(gate)
    hidden = (swish * upper).astype(jnp.bfloat16)
    d_updated = jnp.dot(cotangent, w_head.T, preferred_element_type=jnp.float32)
    d_upd_b = d_updated.astype(jnp.bfloat16)
    d_hidden = jnp.dot(d_upd_b, w_out.T, preferred_element_type=jnp.float32)
    d_gate = (d_hidden * upper * sigma * (1.0 + gate * (1.0 - sigma))).astype(jnp.bfloat16)
    d_up = (d_hidden * swish).astype(jnp.bfloat16)
    d_inputs = jnp.dot(d_gate, w_gate.T, preferred_element_type=jnp.float32) + jnp.dot(
        d_up, w_up.T, preferred_element_type=jnp.float32
    )
    d_norm = (
        d_inputs
        - jnp.mean(d_inputs, axis=-1, keepdims=True)
        - normed * jnp.mean(d_inputs * normed, axis=-1, keepdims=True)
    ) * scale_inv
    d_block = (d_updated + d_norm).astype(jnp.bfloat16)
    terms = (
        jnp.dot(inputs.T, d_gate, preferred_element_type=jnp.float32),
        jnp.dot(inputs.T, d_up, preferred_element_type=jnp.float32),
        jnp.dot(hidden.T, d_upd_b, preferred_element_type=jnp.float32),
        jnp.dot(updated.T, cotangent, preferred_element_type=jnp.float32),
    )
    return (terms, d_block)


def mirror(tile):
    rows, cols, bins = tile.shape
    ncol = lax.axis_size("col")
    nrow = lax.axis_size("row")
    part = rows // ncol
    first = tile.reshape(ncol, part, 2, rows * bins)
    got = lax.all_to_all(first, "col", split_axis=0, concat_axis=0, tiled=True)
    second = jnp.transpose(got, (0, 2, 1, 3)).reshape(nrow, part, rows * bins)
    got = lax.all_to_all(second, "row", split_axis=0, concat_axis=0, tiled=True)
    third = got.reshape(ncol, 2, part, rows * bins)
    got = lax.all_to_all(third, "col", split_axis=0, concat_axis=0, tiled=True)
    result = jnp.transpose(got.reshape(ncol, 2, part, rows, bins), (3, 1, 0, 2, 4))
    return result.reshape(rows, cols, bins)


def body(pair, targets, w_gate, w_up, w_out, w_head):
    rows, cols, width = pair.shape
    bins = w_head.shape[1]
    count = rows * cols
    nblocks = count // count
    blocks = pair.reshape(nblocks, count, width)
    updated, logits = lax.map(lambda blk: forward_block(blk, w_gate, w_up, w_out, w_head), blocks)
    tile = logits.reshape(rows, cols, bins)
    summed = tile.astype(jnp.float32) + mirror(tile).astype(jnp.float32)
    probs = jax.nn.softmax(summed, axis=-1)
    onehot = (targets[:, :, None] == jnp.arange(bins, dtype=jnp.int32)[None, None, :]).astype(
        jnp.float32
    )
    grad_sym = (probs - onehot).astype(jnp.bfloat16)
    cotangent = (grad_sym.astype(jnp.float32) + mirror(grad_sym).astype(jnp.float32)).astype(
        jnp.bfloat16
    )
    cotangent = cotangent.reshape(nblocks, count, bins)

    def accumulate(carry, items):
        flat, upd, cot = items
        terms, d_block = backward_block(flat, upd, cot, w_gate, w_up, w_out, w_head)
        return (tuple((c + t for c, t in zip(carry, terms))), d_block)

    start = (
        jnp.zeros(w_gate.shape, jnp.float32),
        jnp.zeros(w_up.shape, jnp.float32),
        jnp.zeros(w_out.shape, jnp.float32),
        jnp.zeros(w_head.shape, jnp.float32),
    )
    totals, d_blocks = lax.scan(accumulate, start, (blocks, updated, cotangent))
    d_pair = d_blocks.reshape(rows, cols, width)
    partial_sums = (
        lax.psum_scatter(
            totals[0].astype(jnp.bfloat16), "row", scatter_dimension=0, tiled=True
        ).astype(jnp.float32),
        lax.psum_scatter(
            totals[1].astype(jnp.bfloat16), "row", scatter_dimension=0, tiled=True
        ).astype(jnp.float32),
        lax.psum_scatter(
            totals[2].astype(jnp.bfloat16), "row", scatter_dimension=0, tiled=True
        ).astype(jnp.float32),
        lax.psum_scatter(
            totals[3].astype(jnp.bfloat16), "row", scatter_dimension=0, tiled=True
        ).astype(jnp.float32),
    )
    owned = (
        lax.psum_scatter(partial_sums[0], "col", scatter_dimension=1, tiled=True),
        lax.psum_scatter(partial_sums[1], "col", scatter_dimension=1, tiled=True),
        lax.psum_scatter(partial_sums[2], "col", scatter_dimension=1, tiled=True),
        lax.psum_scatter(partial_sums[3], "col", scatter_dimension=1, tiled=True),
    )
    factor = 1.0 / (rows * lax.axis_size("row"))
    return (d_pair, owned[0] * factor, owned[1] * factor, owned[2] * factor, owned[3] * factor)


def solution(mesh):
    placed = (P("row", "col", None), P("row", "col"), P(), P(), P(), P())
    return jax.shard_map(
        body,
        mesh=mesh,
        in_specs=placed,
        out_specs=(
            P("row", "col", None),
            P("row", "col"),
            P("row", "col"),
            P("row", "col"),
            P("row", "col"),
        ),
        check_vma=False,
    )
```

profile of v0, /device:TPU:1, one launch (start us, length us, event | category | flops | bytes accessed | tf_op | source)
XLA Modules:
  0.0 736.5 jit_solution(14181407149266723379)
XLA Ops:
  7.2 1.1 convert_reduce_fusion
  8.3 0.3 multiply_reduce_fusion.1
  8.8 0.2 fusion.3
  9.0 0.7 copy-done.2
  9.7 0.3 fusion.14
  10.0 1.3 multiply_convert_fusion.2
  11.3 0.3 fusion
  11.6 0.4 copy-done.4
  12.4 16.0 %all_to_all.30 = bf16[16,1,2,1024]{3,2,1,0:T(2,128)(2,1)S(1)} all-to-all(bf16[16,1,2,1024]{3,2,1,0:T(2,128)(2,1)S(1)} %bitcast.72), channel_id=1, replica_groups=mesh['row'=32,'col'=16] {'col'}, dimensions={0} | all-to-all | bytes 131072 | tf_op jit(solution)/shard_map/all_to_all | solution.py:66
  28.5 0.5 broadcast.105
  29.0 1.0 reduce.6
  30.0 31.5 %all_to_all.31 = bf16[32,2,512]{2,1,0:T(2,128)(2,1)S(1)} all-to-all(bf16[32,2,512]{2,1,0:T(2,128)(2,1)S(1)} %reshape.206), channel_id=1, replica_groups=mesh['row'=32,'col'=16] {'row'}, dimensions={0} | all-to-all | bytes 131072 | tf_op jit(solution)/shard_map/all_to_all | solution.py:68
  61.5 0.4 reduce.4
  61.9 0.7 reshape.180
  62.6 3.9 all-to-all-start.2
  66.9 6.6 all-to-all-done.2
  75.0 9.7 %all_to_all.32 = bf16[16,1,2,1024]{3,2,1,0:T(2,128)(2,1)S(1)} all-to-all(bf16[16,1,2,1024]{3,2,1,0:T(2,128)(2,1)S(1)} %fusion.10), channel_id=1, replica_groups=mesh['row'=32,'col'=16] {'col'}, dimensions={0} | all-to-all | bytes 131072 | tf_op jit(solution)/shard_map/all_to_all | solution.py:66
  84.8 1.0 reduce.7
  85.8 20.5 %all_to_all.33 = bf16[32,2,512]{2,1,0:T(2,128)(2,1)S(1)} all-to-all(bf16[32,2,512]{2,1,0:T(2,128)(2,1)S(1)} %reshape.208), channel_id=1, replica_groups=mesh['row'=32,'col'=16] {'row'}, dimensions={0} | all-to-all | bytes 131072 | tf_op jit(solution)/shard_map/all_to_all | solution.py:68
  106.4 0.4 reduce.5
  106.7 0.7 reshape.181
  107.4 3.8 all-to-all-start.5
  111.3 1.3 dynamic-slice.1
  112.6 1.3 dynamic-slice.5
  115.8 2.4 all-to-all-done.5
  118.6 0.2 fusion.15
  118.8 1.0 convolution_convert_fusion
  119.8 1.8 multiply_convert_fusion
  121.6 0.9 convolution_convert_fusion.2
  122.5 0.3 fusion.16
  122.9 0.9 convolution_convert_fusion.1
  123.8 0.4 fusion.13
  124.3 1.0 add_convert_fusion
  125.3 0.2 convolution_convert_fusion.4
  125.5 160.1 %all-reduce.3 = bf16[128,64]{1,0:T(8,128)(2,1)S(1)} all-reduce(bf16[128,64]{1,0:T(8,128)(2,1)S(1)} %convolution_convert_fusion.4), channel_id=8, replica_groups=mesh['row'=32,'col'=16] {'row'}, use_global_device_ids=true, to_apply=%region_12.13.clone | all-reduce | flops 8192 | bytes 32768
  285.6 66.1 %all-reduce.5 = (f32[16,128]{1,0:T(8,128)S(1)}, f32[4,64]{1,0:T(4,128)S(1)}) all-reduce(bf16[16,128]{1,0:T(8,128)(2,1)} %reduce-scatter.10.cloned.1.call-done, f32[4,64]{1,0:T(4,128)S(1)} %fusion.12), channel_id=7, replica_groups=mesh['row'=32,'col'=16] {'col'}, use_global_device_ids=true, to_apply=%region_11.12.clone | all-reduce | flops 2304 | bytes 14336
  351.8 211.3 %all-reduce.9.cloned.1.call-done = (bf16[128,512]{1,0:T(8,128)(2,1)}, bf16[128,512]{1,0:T(8,128)(2,1)}) async-done(((bf16[128,512]{1,0:T(8,128)(2,1)}, bf16[128,512]{1,0:T(8,128)(2,1)}), (bf16[128,512]{1,0:T(8,128)(2,1)}, bf16[128,512]{1,0:T(8,128)(2,1)})) %all-reduce.9.cloned.1.call-update) | async-done | bytes 262160
  563.1 0.7 dynamic-slice_convert_fusion
  563.8 0.9 copy.65
  564.7 0.7 dynamic-slice_multiply_fusion.1
  565.4 0.7 copy.61
  566.1 0.8 copy.63
  566.9 72.9 %reduce-scatter.14.cloned.1.call-done = f32[32,4]{1,0:T(8,128)} async-done(((f32[512,4]{1,0:T(8,128)}), f32[32,4]{1,0:T(8,128)}) %reduce-scatter.14.cloned.1.call-update) | async-done | bytes 528
  639.9 0.8 copy.66
  640.7 0.6 broadcast_multiply_fusion.1
  641.3 87.3 %reduce-scatter.12.cloned.1.call-done = f32[32,4]{1,0:T(8,128)} async-done(((f32[512,4]{1,0:T(8,128)}), f32[32,4]{1,0:T(8,128)}) %reduce-scatter.12.cloned.1.call-update) | async-done | bytes 528
  728.6 0.8 copy.64
  729.4 0.6 broadcast_multiply_fusion.2
  (59 shorter events, 3.5 us)
Async XLA Ops:
  7.2 2.8 copy-start
  7.2 1.1 copy-start.1
  8.8 0.9 copy-start.2
  9.9 1.3 copy-start.3
  11.3 0.7 copy-start.4
  62.6 3.9 copy-start.5
  62.6 10.9 %all-to-all-start.2 = ((bf16[16,2,1,1024]{3,1,2,0:T(2,128)(2,1)}), bf16[16,2,1,1024]{3,1,2,0:T(2,128)(2,1)S(1)}, u32[]{:S(2)}, u32[]{:S(2)}) async-start(bf16[16,2,1,1024]{3,1,2,0:T(2,128)(2,1)} %bitcast.2), calls=%async_computation.2 | async-start | bytes 131072 | tf_op jit(solution)/shard_map/all_to_all | solution.py:70
  107.4 10.8 %all-to-all-start.5 = ((bf16[16,2,1,1024]{3,1,2,0:T(2,128)(2,1)}), bf16[16,2,1,1024]{3,1,2,0:T(2,128)(2,1)S(1)}, u32[]{:S(2)}, u32[]{:S(2)}) async-start(bf16[16,2,1,1024]{3,1,2,0:T(2,128)(2,1)} %bitcast.6), calls=%async_computation.5 | async-start | bytes 131072 | tf_op jit(solution)/shard_map/all_to_all | solution.py:70
  111.2 174.4 %reduce-scatter.10.cloned.1.call-start = ((), (), s32[]{:S(2)}) async-start(), calls=%async_computation.9 | async-start | bytes 135168 | tf_op jit(solution)/shard_map/reduce_scatter | solution.py:114
  122.8 440.3 %all-reduce.9.cloned.1.call-start = ((), (), s32[]{:S(2)}) async-start(), calls=%async_computation.12 | async-start | bytes 524288
  124.3 515.6 %reduce-scatter.14.cloned.1.call-start = ((), (), s32[]{:S(2)}) async-start(), calls=%async_computation.11 | async-start | bytes 278528
  564.7 163.9 %reduce-scatter.12.cloned.1.call-start = ((), (), s32[]{:S(2)}) async-start(), calls=%async_computation.10 | async-start | bytes 278528
Sparse Core Ops, SparseCore 0:
  123.0 94.3 reduce-scatter.9
  220.3 342.7 all-reduce.8
  565.9 73.9 reduce-scatter.13
  642.5 86.0 reduce-scatter.11
where the time goes:
time: 749 us; the launch traced here: 737 us
  waiting for transfers between devices  381 us (51%)
  blocking collectives  304 us (41%)
  between operations  16 us (2%)
  local copies, waits for them, and re-layouts  12 us (2%)
  other arithmetic  8.33 us (1%)
  starting transfers between devices  7.9 us (1%)
  matrix products  7.8 us (1%)
    unnamed x7, waiting for transfers between devices  372 us
    unnamed x2, blocking collectives  226 us
    all_to_all x2, blocking collectives, mirror(): got = lax.all_to_all(second, 'row', split_axis=0, concat_axis=0, tiled=True)  52 us
    all_to_all x2, blocking collectives, mirror(): got = lax.all_to_all(first, 'col', split_axis=0, concat_axis=0, tiled=True)  25.7 us
  transfers between devices with their start and end apart: 6, of which 5 were waited for; matrix products, arithmetic and copies ran while one was open for 1% of the time, Pallas kernels for 0%

commit v1 on v0

v1 whole, which is shorter than its diff:
```python
import functools

import jax
import jax.numpy as jnp
from jax import lax
from jax.experimental import pallas as pl
from jax.experimental.pallas import tpu as pltpu
from jax.sharding import PartitionSpec as P

MESH = pl.DeviceIdType.MESH
F32 = jnp.float32
BF16 = jnp.bfloat16
eps = 1e-05

NX = NY = NZH = NZL = 4
XY_ORDER = sorted(
    range(1, 16), key=lambda k: -(min(k // 4, 4 - k // 4) + min(k % 4, 4 - k % 4))
)
Z_ORDER = sorted(range(1, 16), key=lambda k: -min(k, 16 - k))


def nn(a, b):
    return jnp.dot(a, b, preferred_element_type=F32)


def nt(a, b):
    return lax.dot_general(a, b, (((1,), (1,)), ((), ())), preferred_element_type=F32)


def tn(a, b):
    return lax.dot_general(a, b, (((0,), (0,)), ((), ())), preferred_element_type=F32)


def kernel(
    pair_in,
    tgt_in,
    wg_in,
    wu_in,
    wo_in,
    wh_in,
    dp_out,
    gg_out,
    gu_out,
    go_out,
    gh_out,
    pv,
    tv,
    wg,
    wu,
    wo,
    wh,
    wdup,
    inp,
    normed,
    sinv,
    hidden,
    swish,
    slope,
    upd,
    logit,
    mbuf,
    mrecv,
    onehot,
    cot,
    dupd,
    dupb,
    dgate,
    dup,
    dpv,
    part,
    crecv,
    xbuf,
    xrecv,
    red,
    zbuf,
    zrecv,
    fin,
    fint,
    in_sem,
    ms,
    mr,
    cs,
    cr,
    xs,
    xr,
    zs,
    zr,
    fs,
    fr,
    out_sem,
):
    r = lax.axis_index("row")
    c = lax.axis_index("col")
    x, zh, core = r // 8, (r // 2) % 4, r % 2
    y, zl = c // 4, c % 4
    z = zh * 4 + zl
    diag = c == r // 2
    other = (r + 1 - 2 * core, c)

    loads = [
        pltpu.make_async_copy(src, dst, in_sem.at[n])
        for n, (src, dst) in enumerate(
            ((pair_in, pv), (wg_in, wg), (wu_in, wu), (wo_in, wo), (wh_in, wh), (tgt_in, tv))
        )
    ]
    for load in loads:
        load.start()

    def xy_dev(k):
        return ((x + k // 4) % 4 * 8 + zh * 2 + core, (y + k % 4) % 4 * 4 + zl)

    def z_dev(k):
        to = (z + k) % 16
        return (x * 8 + to // 4 * 2 + core, y * 4 + to % 4)

    barrier = pltpu.get_barrier_semaphore()

    def greet(dev):
        pl.semaphore_signal(barrier, inc=1, device_id=dev, device_id_type=MESH)

    for h in range(2):
        pl.when(jnp.logical_not(jnp.logical_and(diag, core == h)))(
            functools.partial(greet, (2 * c + h, r // 2))
        )
    for k in Z_ORDER:
        greet(z_dev(k))
    for k in XY_ORDER:
        greet(xy_dev(k))
    greet(other)

    lane = lax.broadcasted_iota(jnp.int32, (256, 128), 1)
    prow = lax.broadcasted_iota(jnp.int32, (256, 128), 0)

    for load in loads:
        load.wait()
    dup_sel = (
        lax.broadcasted_iota(jnp.int32, (64, 128), 1) % 64
        == lax.broadcasted_iota(jnp.int32, (64, 128), 0)
    ).astype(BF16)
    wdup[...] = nn(wh[...], dup_sel).astype(BF16)
    for h in range(2):
        rows = pl.ds(h * 256, 256)
        v = pv[:, h * 16 : (h + 1) * 16, :].reshape(256, 128).astype(F32)
        centre = v - jnp.mean(v, axis=-1, keepdims=True)
        scale = lax.rsqrt(jnp.mean(centre * centre, axis=-1, keepdims=True) + eps)
        nrm = centre * scale
        normed[rows, :] = nrm
        sinv[rows, :] = jnp.broadcast_to(scale, (256, 128))
        inputs = nrm.astype(BF16)
        inp[rows, :] = inputs
        for n in range(2):
            cols = slice(n * 256, (n + 1) * 256)
            gate = nn(inputs, wg[:, cols])
            upper = nn(inputs, wu[:, cols])
            sigma = 0.5 * jnp.tanh(0.5 * gate) + 0.5
            sw = gate * sigma
            hidden[rows, cols] = (sw * upper).astype(BF16)
            swish[rows, cols] = sw
            slope[rows, cols] = upper * sigma * (1.0 + gate * (1.0 - sigma))
        updated = (v + nn(hidden[rows, :], wo[...])).astype(BF16)
        upd[rows, :] = updated
        lg = nn(updated, wdup[...])
        logit[rows, :] = lg.astype(BF16).astype(F32)
        mbuf[h] = jnp.where(lane[:128] < 64, lg[:128], lg[128:]).astype(BF16)

    pl.semaphore_wait(barrier, 33 - diag.astype(jnp.int32))

    def mirror_copy(h, slot):
        return pltpu.make_async_remote_copy(
            src_ref=mbuf.at[h],
            dst_ref=mrecv.at[slot],
            send_sem=ms.at[h],
            recv_sem=mr.at[slot],
            device_id=(2 * c + h, r // 2),
            device_id_type=MESH,
        )

    for h in range(2):
        here = jnp.logical_and(diag, core == h)

        @pl.when(jnp.logical_not(here))
        def _():
            mirror_copy(h, core).start()

        @pl.when(here)
        def _():
            mrecv[h] = mbuf[h]

    jj = prow % 16
    valid = (lane // 64) == (jj // 8)
    spread = (
        lax.broadcasted_iota(jnp.int32, (256, 16), 0) // 16
        == lax.broadcasted_iota(jnp.int32, (256, 16), 1)
    ).astype(BF16)
    by_row = nn(spread, tv[...].astype(F32).astype(BF16))
    at = lax.broadcasted_iota(jnp.int32, (256, 32), 0) % 16
    lane32 = lax.broadcasted_iota(jnp.int32, (256, 32), 1)
    ones = jnp.ones((32, 128), BF16)
    for h in range(2):
        picked = jnp.where(lane32 == at + h * 16, by_row, 0.0).astype(BF16)
        target = nn(picked, ones)
        onehot[h * 256 : (h + 1) * 256, :] = jnp.where(
            jnp.logical_and(valid, (lane % 64).astype(F32) == target), 1.0, 0.0
        )
    perm = (lane == (jj % 8) * 16 + prow // 16).astype(BF16)
    for d in range(16):
        part[1, d, 48:64, :] = jnp.zeros((16, 128), BF16)

    for h in range(2):
        here = jnp.logical_and(diag, core == h)

        @pl.when(jnp.logical_not(here))
        def _():
            mirror_copy(h, h).wait_recv()

        rows = pl.ds(h * 256, 256)
        total = jnp.where(valid, logit[rows, :] + nn(perm, mrecv[h]), -1e30)
        shifted = jnp.exp(total - jnp.max(total, axis=-1, keepdims=True))
        probs = shifted / jnp.sum(shifted, axis=-1, keepdims=True)
        grad = (probs - onehot[rows, :]).astype(BF16).astype(F32)
        cotangent = (grad + grad).astype(BF16)
        cot[rows, :] = cotangent
        d_updated = nt(cotangent, wdup[...])
        dupd[rows, :] = d_updated
        d_upd_b = d_updated.astype(BF16)
        dupb[rows, :] = d_upd_b

    g_head = tn(upd[...], cot[...])
    g_head = g_head + pltpu.roll(g_head, 64, 1)
    for a in range(4):
        packed = jnp.where(
            lane[:16] < 64, g_head[32 * a : 32 * a + 16], g_head[32 * a + 16 : 32 * a + 32]
        ).astype(BF16)
        for b in range(4):
            part[1, a * 4 + b, 32:48, :] = packed
    for a in range(4):
        g_out = tn(dupb[...], hidden[:, a * 128 : (a + 1) * 128]).astype(BF16)
        for b in range(4):
            part[1, a * 4 + b, 0:32, :] = g_out[32 * b : 32 * b + 32]

    core_copy = pltpu.make_async_remote_copy(
        src_ref=part.at[1 - core],
        dst_ref=crecv,
        send_sem=cs,
        recv_sem=cr,
        device_id=other,
        device_id_type=MESH,
    )
    pl.when(core == 0)(core_copy.start)

    for h in range(2):
        rows = pl.ds(h * 256, 256)
        for n in range(2):
            cols = slice(n * 256, (n + 1) * 256)
            d_hidden = nt(dupb[rows, :], wo[cols, :])
            dgate[rows, cols] = (d_hidden * slope[rows, cols]).astype(BF16)
            dup[rows, cols] = (d_hidden * swish[rows, cols]).astype(BF16)
    for b in range(4):
        cols = slice(b * 128, (b + 1) * 128)
        g_gate = tn(inp[...], dgate[:, cols]).astype(BF16)
        g_up = tn(inp[...], dup[:, cols]).astype(BF16)
        for a in range(4):
            part[0, a * 4 + b, 0:32, :] = g_gate[32 * a : 32 * a + 32]
            part[0, a * 4 + b, 32:64, :] = g_up[32 * a : 32 * a + 32]
    pl.when(core == 1)(core_copy.start)

    core_copy.wait_recv()
    for d in range(16):
        xbuf[d] = (part[core, d].astype(F32) + crecv[d].astype(F32)).astype(BF16)

    def xy_copy(k):
        dev = xy_dev(k)
        to = (x + k // 4) % 4 * 4 + (y + k % 4) % 4
        return pltpu.make_async_remote_copy(
            src_ref=xbuf.at[to],
            dst_ref=xrecv.at[k - 1],
            send_sem=xs.at[k - 1],
            recv_sem=xr.at[k - 1],
            device_id=dev,
            device_id_type=MESH,
        )

    xy_copies = {k: xy_copy(k) for k in XY_ORDER}
    for k in XY_ORDER:
        xy_copies[k].start()

    for h in range(2):
        rows = pl.ds(h * 256, 256)
        d_inputs = nt(dgate[rows, :], wg[...]) + nt(dup[rows, :], wu[...])
        nrm = normed[rows, :]
        d_norm = (
            d_inputs
            - jnp.mean(d_inputs, axis=-1, keepdims=True)
            - nrm * jnp.mean(d_inputs * nrm, axis=-1, keepdims=True)
        ) * sinv[rows, :]
        dpv[:, h * 16 : (h + 1) * 16, :] = (
            (dupd[rows, :] + d_norm).astype(BF16).reshape(16, 16, 128)
        )

    total = xbuf[x * 4 + y].astype(F32)
    for k in reversed(XY_ORDER):
        xy_copies[k].wait_recv()
        total = total + xrecv[k - 1].astype(F32)
    red[...] = total
    for to in range(16):
        first = pl.multiple_of(8 * jnp.where(core == 0, to // 4, to % 4), 8)
        second = pl.multiple_of(32 + 8 * jnp.where(core == 0, to // 4, to // 4 % 2), 8)
        zbuf[to] = jnp.concatenate(
            [red[pl.ds(first, 8), :], red[pl.ds(second, 8), :]], axis=0
        ).astype(BF16)

    def z_copy(k):
        return pltpu.make_async_remote_copy(
            src_ref=zbuf.at[(z + k) % 16],
            dst_ref=zrecv.at[k - 1],
            send_sem=zs.at[k - 1],
            recv_sem=zr.at[k - 1],
            device_id=z_dev(k),
            device_id_type=MESH,
        )

    z_copies = {k: z_copy(k) for k in Z_ORDER}
    for k in Z_ORDER:
        z_copies[k].start()
    store = pltpu.make_async_copy(dpv, dp_out, out_sem)
    store.start()
    total = zbuf[z].astype(F32)
    for k in reversed(Z_ORDER):
        z_copies[k].wait_recv()
        total = total + zrecv[k - 1].astype(F32)
    fin[core] = total * (1.0 / 512.0)

    last = pltpu.make_async_remote_copy(
        src_ref=fin.at[core],
        dst_ref=fin.at[core],
        send_sem=fs,
        recv_sem=fr,
        device_id=other,
        device_id_type=MESH,
    )
    last.start()
    mirror_sends = []
    for h in range(2):
        here = jnp.logical_and(diag, core == h)

        @pl.when(jnp.logical_not(here))
        def _():
            mirror_copy(h, core).wait_send()

    core_copy.wait_send()
    for k in XY_ORDER:
        xy_copies[k].wait_send()
    for k in Z_ORDER:
        z_copies[k].wait_send()
    store.wait()
    last.wait_recv()

    a_tile = pltpu.roll(fin[0], (128 - 32 * zl) % 128, 1)
    b_tile = fin[1]
    gg_out[...] = jnp.where(core == 0, a_tile[0:4, :32], a_tile[4:8, :32])
    gu_out[...] = jnp.where(core == 0, a_tile[8:12, :32], a_tile[12:16, :32])
    fint[...] = jnp.transpose(b_tile[0:8])
    go_out[...] = fint[pl.ds(pl.multiple_of(32 * zh + 16 * core, 16), 16), :]
    h_tile = pltpu.roll(b_tile, (128 - (64 * (zh // 2) + 16 * y + 4 * zl)) % 128, 1)
    gh_out[...] = jnp.where(core == 0, h_tile[8:12, :4], h_tile[12:16, :4])
    last.wait_send()


def body(pair, targets, w_gate, w_up, w_out, w_head):
    vm = pltpu.VMEM
    dma = pltpu.SemaphoreType.DMA
    anywhere = pl.BlockSpec(memory_space=pl.ANY)
    vmem = pl.BlockSpec(memory_space=pltpu.VMEM)
    return pl.pallas_call(
        kernel,
        out_shape=(
            jax.ShapeDtypeStruct((16, 32, 128), BF16),
            jax.ShapeDtypeStruct((4, 32), F32),
            jax.ShapeDtypeStruct((4, 32), F32),
            jax.ShapeDtypeStruct((16, 8), F32),
            jax.ShapeDtypeStruct((4, 4), F32),
        ),
        in_specs=[anywhere] * 6,
        out_specs=(anywhere, vmem, vmem, vmem, vmem),
        scratch_shapes=[
            vm((16, 32, 128), BF16),
            vm((16, 32), jnp.int32),
            vm((128, 512), BF16),
            vm((128, 512), BF16),
            vm((512, 128), BF16),
            vm((128, 64), BF16),
            vm((128, 128), BF16),
            vm((512, 128), BF16),
            vm((512, 128), F32),
            vm((512, 128), F32),
            vm((512, 512), BF16),
            vm((512, 512), F32),
            vm((512, 512), F32),
            vm((512, 128), BF16),
            vm((512, 128), F32),
            vm((2, 128, 128), BF16),
            vm((2, 128, 128), BF16),
            vm((512, 128), F32),
            vm((512, 128), BF16),
            vm((512, 128), F32),
            vm((512, 128), BF16),
            vm((512, 512), BF16),
            vm((512, 512), BF16),
            vm((16, 32, 128), BF16),
            vm((2, 16, 64, 128), BF16),
            vm((16, 64, 128), BF16),
            vm((16, 64, 128), BF16),
            vm((15, 64, 128), BF16),
            vm((64, 128), F32),
            vm((16, 16, 128), BF16),
            vm((15, 16, 128), BF16),
            vm((2, 16, 128), F32),
            vm((128, 8), F32),
            dma((6,)),
            dma((2,)),
            dma((2,)),
            dma,
            dma,
            dma((15,)),
            dma((15,)),
            dma((15,)),
            dma((15,)),
            dma,
            dma,
            dma,
        ],
        compiler_params=pltpu.CompilerParams(collective_id=0, has_side_effects=True),
    )(pair, targets, w_gate, w_up, w_out, w_head)


def solution(mesh):
    placed = (P("row", "col", None), P("row", "col"), P(), P(), P(), P())
    return jax.shard_map(
        body,
        mesh=mesh,
        in_specs=placed,
        out_specs=(
            P("row", "col", None),
            P("row", "col"),
            P("row", "col"),
            P("row", "col"),
            P("row", "col"),
        ),
        check_vma=False,
    )
```

time: 749 us -> 54.8 us (0.07); the launches traced: 737 us -> 54.5 us
  waiting for transfers between devices: 381 us -> 0 us
  blocking collectives: 304 us -> 0 us
  Pallas kernels: 0 us -> 47.5 us
  between operations: 16 us -> 0.65 us
  other arithmetic: 8.33 us -> 0 us
  starting transfers between devices: 7.9 us -> 0 us
  matrix products: 7.8 us -> 0 us
    unnamed x7 -> x0, waiting for transfers between devices: 372 us -> none
    unnamed x2 -> x0, blocking collectives: 226 us -> none
    all_to_all x4 -> x0, blocking collectives: 77.6 us -> none  [the longest x2 52 us: mirror(): got = lax.all_to_all(second, 'row', split_axis=0, concat_axis=0, tiled=True)]
    pallas_call x0 -> x1, Pallas kernels: none -> 47.5 us  [body(): pl.pallas_call(kernel, out_shape=(jax.ShapeDtypeStruct((16, 32, 128), BF1...]
    all_to_all x2 -> x0, waiting for transfers between devices: 9 us -> none  [mirror(): got = lax.all_to_all(third, 'col', split_axis=0, concat_axis=0, tiled=True)]
    dot_general x12 -> x0, matrix products: 7.8 us -> none  [the longest x1 1.81 us: backward_block(): d_hidden = jnp.dot(d_upd_b, w_out.T, preferred_element_type=jnp.float32)]
    all_to_all x2 -> x0, starting transfers between devices: 7.73 us -> none  [mirror(): got = lax.all_to_all(third, 'col', split_axis=0, concat_axis=0, tiled=True)]
  transfers between devices with their start and end apart: 6 -> 0, of which waited for: 5 -> 0; matrix products, arithmetic and copies ran while one was open for 1% -> 0% of each run, Pallas kernels for 0% -> 0%
where the time goes in v1:
time: 54.8 us; the launch traced here: 54.5 us
  Pallas kernels  47.5 us (87%)
  local copies, waits for them, and re-layouts  6.26 us (11%)
  between operations  0.65 us (1%)
    pallas_call x1, Pallas kernels, body(): pl.pallas_call(kernel, out_shape=(jax.ShapeDtypeStruct((16, 32, 128), BF1...  47.5 us
    unnamed x13, local copies, waits for them, and re-layouts  5.6 us

profile of v1, /device:TPU:1, one launch (start us, length us, event | category | flops | bytes accessed | tf_op | source)
XLA Modules:
  0.0 54.5 jit_solution(9752506383298940945)
XLA Ops:
  0.6 1.4 %copy.11.wh_in = bf16[128,64]{1,0:T(8,128)(2,1)} copy(bf16[128,64]{0,1:T(8,128)(2,1)} %param.11) | data formatting | bytes 32768 | tf_op args[5]
  2.1 47.5 %shard_map.101 = (bf16[16,32,128]{2,1,0:T(8,128)(2,1)}, f32[4,32]{1,0:T(4,128)}, f32[4,32]{1,0:T(4,128)}, f32[16,8]{1,0:T(8,128)}, f32[4,4]{1,0:T(4,128)}) custom-call(bf16[16,32,128]{2,1,0:T(8,128)(2,1)} %pair_in.1, s32[16,32]{1,0:T(8,128)} %tgt_in.1, bf16[128,512]{1,0:T(8,128)(2,1)} %wg_in.1, bf16[128,512]{1,0:T(8,128)(2,1)} %wu_in.1, ...), custom_call_target="tpu_custom_call" | custom-call | tf_op jit(solution)/shard_map/pallas_call | solution.py:374
  49.6 0.0 copy-start
  49.6 0.7 %copy-done = f32[16,8]{1,0:T(8,128)S(1)} copy-done((f32[16,8]{1,0:T(8,128)S(1)}, f32[16,8]{1,0:T(8,128)}, u32[]{:S(2)}) %copy-start) | copy-done | bytes 536
  50.3 0.7 %copy.12 = f32[16,8]{0,1:T(8,128)} copy(f32[16,8]{1,0:T(8,128)S(1)} %copy-done) | data formatting | bytes 1024 | tf_op jit(solution)/shard_map/pallas_call | solution.py:374
  51.0 0.0 copy-start.3
  51.0 1.6 %copy.17 = bf16[16,32,128]{2,1,0:T(8,128)(2,1)} copy(bf16[16,32,128]{2,1,0:T(8,128)(2,1)} %get-tuple-element.15) | data formatting | bytes 262144
  52.5 0.0 copy-done.3
  52.5 0.0 copy-start.2
  52.5 0.6 %copy.18 = f32[4,32]{1,0:T(4,128)} copy(f32[4,32]{1,0:T(4,128)S(1)} %copy-done.3) | data formatting | bytes 1024
  53.1 0.1 copy-done.2
  53.2 0.0 copy-start.1
  53.2 0.6 %copy.19 = f32[4,32]{1,0:T(4,128)} copy(f32[4,32]{1,0:T(4,128)S(1)} %copy-done.2) | data formatting | bytes 1024
  53.8 0.1 copy-done.1
  53.9 0.6 %copy.20 = f32[4,4]{1,0:T(4,128)} copy(f32[4,4]{1,0:T(4,128)S(1)} %copy-done.1) | data formatting | bytes 128
Async XLA Ops:
  49.6 0.7 %copy-start = (f32[16,8]{1,0:T(8,128)S(1)}, f32[16,8]{1,0:T(8,128)}, u32[]{:S(2)}) copy-start(f32[16,8]{1,0:T(8,128)} %get-tuple-element.8) | copy-start | bytes 1540
  51.0 1.6 %copy-start.3 = (f32[4,32]{1,0:T(4,128)S(1)}, f32[4,32]{1,0:T(4,128)}, u32[]{:S(2)}) copy-start(f32[4,32]{1,0:T(4,128)} %get-tuple-element.16) | copy-start | bytes 1540
  52.5 0.7 %copy-start.2 = (f32[4,32]{1,0:T(4,128)S(1)}, f32[4,32]{1,0:T(4,128)}, u32[]{:S(2)}) copy-start(f32[4,32]{1,0:T(4,128)} %get-tuple-element.17) | copy-start | bytes 1540
  53.2 0.7 %copy-start.1 = (f32[4,4]{1,0:T(4,128)S(1)}, f32[4,4]{1,0:T(4,128)}, u32[]{:S(2)}) copy-start(f32[4,4]{1,0:T(4,128)} %get-tuple-element.19) | copy-start | bytes 196

commit v2 on v1

v2 whole, which is shorter than its diff:
```python
import functools

import jax
import jax.numpy as jnp
from jax import lax
from jax.experimental import pallas as pl
from jax.experimental.pallas import tpu as pltpu
from jax.sharding import PartitionSpec as P

MESH = pl.DeviceIdType.MESH
F32 = jnp.float32
BF16 = jnp.bfloat16
eps = 1e-05

NX = NY = NZH = NZL = 4
XY_ORDER = sorted(
    range(1, 16), key=lambda k: -(min(k // 4, 4 - k // 4) + min(k % 4, 4 - k % 4))
)
Z_ORDER = sorted(
    [(k, q) for k in range(16) for q in range(2) if k + q > 0], key=lambda p: -min(p[0], 16 - p[0])
)


def nn(a, b):
    return jnp.dot(a, b, preferred_element_type=F32)


def nt(a, b):
    return lax.dot_general(a, b, (((1,), (1,)), ((), ())), preferred_element_type=F32)


def tn(a, b):
    return lax.dot_general(a, b, (((0,), (0,)), ((), ())), preferred_element_type=F32)


def kernel(
    pair_in,
    tgt_in,
    wg_in,
    wu_in,
    wo_in,
    wh_in,
    dp_out,
    fin_out,
    pv,
    tv,
    wg,
    wu,
    wo,
    wdup,
    wdup_t,
    wo_t,
    inp,
    inp_t,
    normed,
    sinv,
    hidden,
    swish,
    slope,
    upd,
    upd_t,
    logit,
    mbuf,
    mrecv,
    onehot,
    cot,
    dupd,
    dupb,
    dupb_t,
    dgate,
    dup,
    part,
    crecv,
    xbuf,
    xrecv,
    red,
    zbuf,
    zrecv,
    in_sem,
    ms,
    mr,
    cs,
    cr,
    xs,
    xr,
    zs,
    zr,
):
    r = lax.axis_index("row")
    c = lax.axis_index("col")
    x, zh, core = r // 8, (r // 2) % 4, r % 2
    y, zl = c // 4, c % 4
    z = zh * 4 + zl
    diag = c == r // 2
    other = (r + 1 - 2 * core, c)

    loads = [
        pltpu.make_async_copy(src, dst, in_sem.at[n])
        for n, (src, dst) in enumerate(
            ((pair_in, pv), (wg_in, wg), (wu_in, wu), (wo_in, wo), (wh_in, wdup_t.at[0:64]), (tgt_in, tv))
        )
    ]
    for load in loads:
        load.start()

    def xy_dev(k):
        return ((x + k // 4) % 4 * 8 + zh * 2 + core, (y + k % 4) % 4 * 4 + zl)

    def z_dev(k, q):
        to = (z + k) % 16
        return (x * 8 + to // 4 * 2 + (core + q) % 2, y * 4 + to % 4)

    barrier = pltpu.get_barrier_semaphore()

    def greet(dev):
        pl.semaphore_signal(barrier, inc=1, device_id=dev, device_id_type=MESH)

    for h in range(2):
        pl.when(jnp.logical_not(jnp.logical_and(diag, core == h)))(
            functools.partial(greet, (2 * c + h, r // 2))
        )
    for k, q in Z_ORDER:
        greet(z_dev(k, q))
    for k in XY_ORDER:
        greet(xy_dev(k))

    lane = lax.broadcasted_iota(jnp.int32, (256, 128), 1)
    prow = lax.broadcasted_iota(jnp.int32, (256, 128), 0)

    for load in loads:
        load.wait()
    wdup_t[64:128, :] = wdup_t[0:64, :]
    for h in range(2):
        rows = pl.ds(h * 256, 256)
        v = pv[:, h * 16 : (h + 1) * 16, :].reshape(256, 128).astype(F32)
        centre = v - jnp.mean(v, axis=-1, keepdims=True)
        scale = lax.rsqrt(jnp.mean(centre * centre, axis=-1, keepdims=True) + eps)
        nrm = centre * scale
        normed[rows, :] = nrm
        sinv[rows, :] = jnp.broadcast_to(scale, (256, 128))
        inputs = nrm.astype(BF16)
        inp[rows, :] = inputs
        for n in range(2):
            cols = slice(n * 256, (n + 1) * 256)
            gate = nn(inputs, wg[:, cols])
            upper = nn(inputs, wu[:, cols])
            sigma = 0.5 * jnp.tanh(0.5 * gate) + 0.5
            sw = gate * sigma
            hidden[rows, cols] = (sw * upper).astype(BF16)
            swish[rows, cols] = sw
            slope[rows, cols] = upper * sigma * (1.0 + gate * (1.0 - sigma))
        updated = (v + nn(hidden[rows, :], wo[...])).astype(BF16)
        upd[rows, :] = updated
        lg = nt(updated, wdup_t[...])
        logit[rows, :] = lg.astype(BF16).astype(F32)
        mbuf[h] = jnp.where(lane[:128] < 64, lg[:128], lg[128:]).astype(BF16)

    pl.semaphore_wait(barrier, 48 - diag.astype(jnp.int32))

    def mirror_copy(h, slot):
        return pltpu.make_async_remote_copy(
            src_ref=mbuf.at[h],
            dst_ref=mrecv.at[slot],
            send_sem=ms.at[h],
            recv_sem=mr.at[slot],
            device_id=(2 * c + h, r // 2),
            device_id_type=MESH,
        )

    for h in range(2):
        here = jnp.logical_and(diag, core == h)

        @pl.when(jnp.logical_not(here))
        def _():
            mirror_copy(h, core).start()

        @pl.when(here)
        def _():
            mrecv[h] = mbuf[h]

    jj = prow % 16
    valid = (lane // 64) == (jj // 8)
    spread = (
        lax.broadcasted_iota(jnp.int32, (256, 16), 0) // 16
        == lax.broadcasted_iota(jnp.int32, (256, 16), 1)
    ).astype(BF16)
    by_row = nn(spread, tv[...].astype(F32).astype(BF16))
    at = lax.broadcasted_iota(jnp.int32, (256, 32), 0) % 16
    lane32 = lax.broadcasted_iota(jnp.int32, (256, 32), 1)
    ones = jnp.ones((32, 128), BF16)
    for h in range(2):
        picked = jnp.where(lane32 == at + h * 16, by_row, 0.0).astype(BF16)
        target = nn(picked, ones)
        onehot[h * 256 : (h + 1) * 256, :] = jnp.where(
            jnp.logical_and(valid, (lane % 64).astype(F32) == target), 1.0, 0.0
        )
    wdup[...] = jnp.transpose(wdup_t[...])
    wo_t[...] = jnp.transpose(wo[...])
    inp_t[...] = jnp.transpose(inp[...])
    upd_t[...] = jnp.transpose(upd[...])
    perm = (lane == (jj % 8) * 16 + prow // 16).astype(BF16)
    for d in range(16):
        part[1, d, 48:64, :] = jnp.zeros((16, 128), BF16)

    for h in range(2):
        here = jnp.logical_and(diag, core == h)

        @pl.when(jnp.logical_not(here))
        def _():
            mirror_copy(h, h).wait_recv()

        rows = pl.ds(h * 256, 256)
        total = jnp.where(valid, logit[rows, :] + nn(perm, mrecv[h]), -1e30)
        shifted = jnp.exp(total - jnp.max(total, axis=-1, keepdims=True))
        probs = shifted / jnp.sum(shifted, axis=-1, keepdims=True)
        grad = (probs - onehot[rows, :]).astype(BF16).astype(F32)
        cotangent = (grad + grad).astype(BF16)
        cot[rows, :] = cotangent
        d_updated = nn(cotangent, wdup_t[...])
        dupd[rows, :] = d_updated
        dupb[rows, :] = d_updated.astype(BF16)

    core_copy = pltpu.make_async_remote_copy(
        src_ref=part.at[1 - core],
        dst_ref=crecv,
        send_sem=cs,
        recv_sem=cr,
        device_id=other,
        device_id_type=MESH,
    )

    def out_and_head():
        dupb_t[...] = nt(wdup[...], cot[...]).astype(BF16)
        g_head = nn(upd_t[...], cot[...])
        g_head = g_head + pltpu.roll(g_head, 64, 1)
        for a in range(4):
            packed = jnp.where(
                lane[:16] < 64, g_head[32 * a : 32 * a + 16], g_head[32 * a + 16 : 32 * a + 32]
            ).astype(BF16)
            for b in range(4):
                part[1, a * 4 + b, 32:48, :] = packed
        for a in range(4):
            g_out = nn(dupb_t[...], hidden[:, a * 128 : (a + 1) * 128]).astype(BF16)
            for b in range(4):
                part[1, a * 4 + b, 0:32, :] = g_out[32 * b : 32 * b + 32]

    def gate_and_up():
        for h in range(2):
            rows = pl.ds(h * 256, 256)
            for n in range(2):
                cols = slice(n * 256, (n + 1) * 256)
                d_hidden = nn(dupb[rows, :], wo_t[:, cols])
                dgate[rows, cols] = (d_hidden * slope[rows, cols]).astype(BF16)
                dup[rows, cols] = (d_hidden * swish[rows, cols]).astype(BF16)
        for b in range(4):
            cols = slice(b * 128, (b + 1) * 128)
            g_gate = nn(inp_t[...], dgate[:, cols]).astype(BF16)
            g_up = nn(inp_t[...], dup[:, cols]).astype(BF16)
            for a in range(4):
                part[0, a * 4 + b, 0:32, :] = g_gate[32 * a : 32 * a + 32]
                part[0, a * 4 + b, 32:64, :] = g_up[32 * a : 32 * a + 32]

    @pl.when(core == 0)
    def _():
        out_and_head()
        core_copy.start()
        gate_and_up()

    @pl.when(core == 1)
    def _():
        gate_and_up()
        core_copy.start()
        out_and_head()

    core_copy.wait_recv()
    for d in range(16):
        xbuf[d] = (part[core, d].astype(F32) + crecv[d].astype(F32)).astype(BF16)

    def xy_copy(k):
        dev = xy_dev(k)
        to = (x + k // 4) % 4 * 4 + (y + k % 4) % 4
        return pltpu.make_async_remote_copy(
            src_ref=xbuf.at[to],
            dst_ref=xrecv.at[k - 1],
            send_sem=xs.at[k - 1],
            recv_sem=xr.at[k - 1],
            device_id=dev,
            device_id_type=MESH,
        )

    xy_copies = {k: xy_copy(k) for k in XY_ORDER}
    for k in XY_ORDER:
        xy_copies[k].start()

    for h in range(2):
        rows = pl.ds(h * 256, 256)
        d_inputs = nt(dgate[rows, :], wg[...]) + nt(dup[rows, :], wu[...])
        nrm = normed[rows, :]
        d_norm = (
            d_inputs
            - jnp.mean(d_inputs, axis=-1, keepdims=True)
            - nrm * jnp.mean(d_inputs * nrm, axis=-1, keepdims=True)
        ) * sinv[rows, :]
        dp_out[:, h * 16 : (h + 1) * 16, :] = (
            (dupd[rows, :] + d_norm).astype(BF16).reshape(16, 16, 128)
        )

    total = xbuf[x * 4 + y].astype(F32)
    for k in reversed(XY_ORDER):
        xy_copies[k].wait_recv()
        total = total + xrecv[k - 1].astype(F32)
    red[...] = total
    half = lane[:8] // 64
    for to in range(16):
        own = jnp.where(core == 0, to // 4, to % 4)
        keep = jnp.where(core == 0, to % 4 // 2, to // 4 // 2)
        first = pl.multiple_of(8 * own, 8)
        second = pl.multiple_of(32 + 8 * jnp.where(core == 0, to // 4, to // 4 % 2), 8)
        zbuf[to] = jnp.where(
            half == keep, red[pl.ds(first, 8), :], pltpu.roll(red[pl.ds(second, 8), :], 64, 1)
        ).astype(BF16)

    def z_copy(k, q):
        return pltpu.make_async_remote_copy(
            src_ref=zbuf.at[(z + k) % 16],
            dst_ref=zrecv.at[core, k],
            send_sem=zs.at[q, k],
            recv_sem=zr.at[core, k],
            device_id=z_dev(k, q),
            device_id_type=MESH,
        )

    def z_arrival(k, p):
        return pltpu.make_async_remote_copy(
            src_ref=zbuf.at[k],
            dst_ref=zrecv.at[p, k],
            send_sem=zs.at[0, k],
            recv_sem=zr.at[p, k],
            device_id=other,
            device_id_type=MESH,
        )

    z_copies = [z_copy(k, q) for k, q in Z_ORDER]
    for copy in z_copies:
        copy.start()
    zrecv[core, 0] = zbuf[z]
    z_arrival(0, 1 - core).wait_recv()
    total = zrecv[:, 0].astype(F32)
    for k in sorted(range(1, 16), key=lambda k: min(k, 16 - k)):
        z_arrival(k, 0).wait_recv()
        z_arrival(k, 1).wait_recv()
        total = total + zrecv[:, k].astype(F32)
    fin_out[...] = total * (1.0 / 512.0)

    for h in range(2):
        here = jnp.logical_and(diag, core == h)

        @pl.when(jnp.logical_not(here))
        def _():
            mirror_copy(h, core).wait_send()

    core_copy.wait_send()
    for k in XY_ORDER:
        xy_copies[k].wait_send()
    for copy in z_copies:
        copy.wait_send()


def finish(dp_in, fin, dp_out, gg_out, gu_out, go_out, gh_out, sem):
    store = pltpu.make_async_copy(dp_in, dp_out, sem)
    store.start()
    r = lax.axis_index("row")
    c = lax.axis_index("col")
    zh, core, y, zl = (r // 2) % 4, r % 2, c // 4, c % 4
    a_tile = pltpu.roll(fin[0], (128 - 32 * zl) % 128, 1)
    gg_out[...] = jnp.where(core == 0, a_tile[0:4, 0:32], a_tile[4:8, 0:32])
    gu_out[...] = jnp.where(core == 0, a_tile[0:4, 64:96], a_tile[4:8, 64:96])
    b_tile = fin[1]
    go_out[...] = pltpu.roll(b_tile, (128 - (32 * zh + 16 * core)) % 128, 1)[:, :16]
    h_tile = pltpu.roll(b_tile, (192 - (64 * (zh // 2) + 16 * y + 4 * zl)) % 128, 1)
    gh_out[...] = jnp.where(core == 0, h_tile[0:4, :4], h_tile[4:8, :4])
    store.wait()


def body(pair, targets, w_gate, w_up, w_out, w_head):
    vm = pltpu.VMEM
    dma = pltpu.SemaphoreType.DMA
    anywhere = pl.BlockSpec(memory_space=pl.ANY)
    vmem = pl.BlockSpec(memory_space=pltpu.VMEM)
    d_pair, fin = pl.pallas_call(
        kernel,
        out_shape=(
            pltpu.VMEM((16, 32, 128), BF16),
            pltpu.VMEM((2, 8, 128), F32),
        ),
        in_specs=[anywhere] * 6,
        out_specs=(vmem, vmem),
        scratch_shapes=[
            vm((16, 32, 128), BF16),
            vm((16, 32), jnp.int32),
            vm((128, 512), BF16),
            vm((128, 512), BF16),
            vm((512, 128), BF16),
            vm((128, 128), BF16),
            vm((128, 128), BF16),
            vm((128, 512), BF16),
            vm((512, 128), BF16),
            vm((128, 512), BF16),
            vm((512, 128), F32),
            vm((512, 128), F32),
            vm((512, 512), BF16),
            vm((512, 512), F32),
            vm((512, 512), F32),
            vm((512, 128), BF16),
            vm((128, 512), BF16),
            vm((512, 128), F32),
            vm((2, 128, 128), BF16),
            vm((2, 128, 128), BF16),
            vm((512, 128), F32),
            vm((512, 128), BF16),
            vm((512, 128), F32),
            vm((512, 128), BF16),
            vm((128, 512), BF16),
            vm((512, 512), BF16),
            vm((512, 512), BF16),
            vm((2, 16, 64, 128), BF16),
            vm((16, 64, 128), BF16),
            vm((16, 64, 128), BF16),
            vm((15, 64, 128), BF16),
            vm((64, 128), F32),
            vm((16, 8, 128), BF16),
            vm((2, 16, 8, 128), BF16),
            dma((6,)),
            dma((2,)),
            dma((2,)),
            dma,
            dma,
            dma((15,)),
            dma((15,)),
            dma((2, 16)),
            dma((2, 16)),
        ],
        compiler_params=pltpu.CompilerParams(
            collective_id=0, has_side_effects=True
        ),
    )(pair, targets, w_gate, w_up, w_out, w_head.T)
    d_pair, g_gate, g_up, g_out, g_head = pl.pallas_call(
        finish,
        out_shape=(
            jax.ShapeDtypeStruct((16, 32, 128), BF16),
            jax.ShapeDtypeStruct((4, 32), F32),
            jax.ShapeDtypeStruct((4, 32), F32),
            jax.ShapeDtypeStruct((8, 16), F32),
            jax.ShapeDtypeStruct((4, 4), F32),
        ),
        in_specs=[vmem, vmem],
        out_specs=(anywhere, vmem, vmem, vmem, vmem),
        scratch_shapes=[dma],
        compiler_params=pltpu.CompilerParams(vmem_limit_bytes=16 * 2**20),
    )(d_pair, fin)
    return d_pair, g_gate, g_up, g_out.T, g_head


def solution(mesh):
    placed = (P("row", "col", None), P("row", "col"), P(), P(), P(), P())
    return jax.shard_map(
        body,
        mesh=mesh,
        in_specs=placed,
        out_specs=(
            P("row", "col", None),
            P("row", "col"),
            P("row", "col"),
            P("row", "col"),
            P("row", "col"),
        ),
        check_vma=False,
    )
```

time: 54.8 us -> 48 us (0.88)
  local copies, waits for them, and re-layouts: 6.26 us -> 0 us
    unnamed x13 -> x0, local copies, waits for them, and re-layouts: 5.6 us -> none
    pallas_call x1 -> x0, local copies, waits for them, and re-layouts: 0.66 us -> none  [body(): pl.pallas_call(kernel, out_shape=(jax.ShapeDtypeStruct((16, 32, 128), BF1...]
    pallas_call x1 -> x2, Pallas kernels: 47.5 us -> 47.2 us  [the longest x1 45.9 us: body(): pl.pallas_call(kernel, out_shape=(pltpu.VMEM((16, 32, 128), BF16), pltpu....]
where the time goes in v2:
time: 48 us; the launch traced here: 47.8 us
  Pallas kernels  47.2 us (98%)
  between operations  0.64 us (1%)
    pallas_call x1, Pallas kernels, body(): pl.pallas_call(kernel, out_shape=(pltpu.VMEM((16, 32, 128), BF16), pltpu....  45.9 us
    pallas_call x1, Pallas kernels, body(): pl.pallas_call(finish, out_shape=(jax.ShapeDtypeStruct((16, 32, 128), BF1...  1.3 us

profile of v2, /device:TPU:1, one launch (start us, length us, event | category | flops | bytes accessed | tf_op | source)
XLA Modules:
  0.0 47.8 jit_solution(31986974330329045)
XLA Ops:
  0.6 45.9 %shard_map.101 = (bf16[16,32,128]{2,1,0:T(8,128)(2,1)S(1)}, f32[2,8,128]{2,1,0:T(8,128)S(1)}) custom-call(bf16[16,32,128]{2,1,0:T(8,128)(2,1)} %pair_in.1, s32[16,32]{1,0:T(8,128)} %tgt_in.1, bf16[128,512]{1,0:T(8,128)(2,1)} %wg_in.1, bf16[128,512]{1,0:T(8,128)(2,1)} %wu_in.1, bf16[512,128]{1,0:T(8,128)(2,1)} %wo_in.1, bf16[64,128]{1,0:T(8,128)(2,1)} %bitcast.2), custom_call_target="tpu_custom_call" | custom-call | tf_op jit(solution)/shard_map/pallas_call | solution.py:390
  46.5 1.3 %shard_map.102 = (bf16[16,32,128]{2,1,0:T(8,128)(2,1)}, f32[4,32]{1,0:T(4,128)}, f32[4,32]{1,0:T(4,128)}, f32[8,16]{1,0:T(8,128)}, f32[4,4]{1,0:T(4,128)}) custom-call(bf16[16,32,128]{2,1,0:T(8,128)(2,1)S(1)} %get-tuple-element.12.dp_in, f32[2,8,128]{2,1,0:T(8,128)S(1)} %get-tuple-element.13.fin), custom_call_target="tpu_custom_call" | custom-call | tf_op jit(solution)/shard_map/pallas_call | solution.py:447

commit v3 on v2

--- a/solution.py
+++ b/solution.py
@@ -19,6 +19,19 @@
 Z_ORDER = sorted(
     [(k, q) for k in range(16) for q in range(2) if k + q > 0], key=lambda p: -min(p[0], 16 - p[0])
 )
+Z_LEVEL = [0, 0, 0, 0, 0, 3, 3, 3, 2, 3, 3, 3, 1, 3, 3, 3]
+Z_MATES = [sum(v <= level for v in Z_LEVEL) - 1 for level in range(4)]
+XY_LIST = sorted(
+    range(16), key=lambda t: (min(t // 4, 4 - t // 4) + min(t % 4, 4 - t % 4), t)
+)
+XY_PLACE = [XY_LIST.index(t) for t in range(16)]
+
+
+def look_up(table, at):
+    found = 0
+    for n, value in enumerate(table):
+        found = jnp.where(at == n, value, found)
+    return found
 
 
 def nn(a, b):
@@ -85,13 +98,28 @@
     xr,
     zs,
     zr,
+    rbuf,
+    rs_send,
+    rs_recv,
+    fw_send,
+    near,
+    along,
+    far,
 ):
     r = lax.axis_index("row")
     c = lax.axis_index("col")
-    x, zh, core = r // 8, (r // 2) % 4, r % 2
-    y, zl = c // 4, c % 4
-    z = zh * 4 + zl
-    diag = c == r // 2
+    chip, core = lax.div(r, 2), lax.rem(r, 2)
+    x, zh = lax.div(chip, 4), lax.rem(chip, 4)
+    y, zl = lax.div(c, 4), lax.rem(c, 4)
+    z, z_swap = zh * 4 + zl, zl * 4 + zh
+    rank, rank_swap = look_up(Z_LEVEL, z), look_up(Z_LEVEL, z_swap)
+    mates = look_up(Z_MATES, rank)
+    place_xy = look_up(XY_PLACE, x * 4 + y)
+    first, late, level = rank < rank_swap, rank > rank_swap, z == z_swap
+    relayed = jnp.logical_and(first, x != y)
+    crossed = jnp.logical_and(z != z_swap, x != y)
+    direct = jnp.logical_and(z != z_swap, jnp.logical_not(first))
+    diag = c == chip
     other = (r + 1 - 2 * core, c)
 
     loads = [
@@ -112,17 +140,46 @@
 
     barrier = pltpu.get_barrier_semaphore()
 
-    def greet(dev):
-        pl.semaphore_signal(barrier, inc=1, device_id=dev, device_id_type=MESH)
-
-    for h in range(2):
-        pl.when(jnp.logical_not(jnp.logical_and(diag, core == h)))(
-            functools.partial(greet, (2 * c + h, r // 2))
-        )
-    for k, q in Z_ORDER:
-        greet(z_dev(k, q))
-    for k in XY_ORDER:
-        greet(xy_dev(k))
+    def tell(sem, dev):
+        pl.semaphore_signal(sem, inc=1, device_id=dev, device_id_type=MESH)
+
+    def wait_some(sem, count):
+        @pl.when(count > 0)
+        def _():
+            pl.semaphore_wait(sem, count)
+
+    def z_mates(t):
+        row = x * 8 + t // 4 * 2
+        return ((row, y * 4 + t % 4), (row + 1, y * 4 + t % 4))
+
+    def xy_mate(t):
+        return (t // 4 * 8 + zh * 2 + core, t % 4 * 4 + zl)
+
+    turned = (y * 8 + zh * 2 + 1 - core, x * 4 + zl)
+
+    @pl.when(jnp.logical_and(crossed, jnp.logical_not(late)))
+    def _():
+        for h in range(2):
+            tell(barrier, (2 * c + h, chip))
+
+    for t in range(16):
+
+        @pl.when(jnp.logical_and(Z_LEVEL[t] >= rank, z != t))
+        def _():
+            for dev in z_mates(t):
+                tell(barrier, dev)
+
+    for t in range(16):
+
+        @pl.when(XY_PLACE[t] > place_xy)
+        def _():
+            tell(barrier, xy_mate(t))
+
+    @pl.when(x < y)
+    def _():
+        tell(barrier, turned)
+
+    tell(barrier, other)
 
     lane = lax.broadcasted_iota(jnp.int32, (256, 128), 1)
     prow = lax.broadcasted_iota(jnp.int32, (256, 128), 0)
@@ -155,7 +212,19 @@
         logit[rows, :] = lg.astype(BF16).astype(F32)
         mbuf[h] = jnp.where(lane[:128] < 64, lg[:128], lg[128:]).astype(BF16)
 
-    pl.semaphore_wait(barrier, 48 - diag.astype(jnp.int32))
+    pl.semaphore_wait(
+        barrier,
+        2 * mates
+        + place_xy
+        + (y < x).astype(jnp.int32)
+        + 1
+        + 2 * jnp.logical_and(crossed, jnp.logical_not(first)).astype(jnp.int32),
+    )
+
+    @pl.when(late)
+    def _():
+        for h in range(2):
+            tell(far, (x * 8 + zl * 2 + h, y * 4 + zh))
 
     def mirror_copy(h, slot):
         return pltpu.make_async_remote_copy(
@@ -163,14 +232,63 @@
             dst_ref=mrecv.at[slot],
             send_sem=ms.at[h],
             recv_sem=mr.at[slot],
-            device_id=(2 * c + h, r // 2),
+            device_id=(2 * c + h, chip),
             device_id_type=MESH,
         )
+
+    def relay_copy(h, slot):
+        return pltpu.make_async_remote_copy(
+            src_ref=mbuf.at[h],
+            dst_ref=rbuf.at[slot],
+            send_sem=rs_send.at[h],
+            recv_sem=rs_recv.at[slot],
+            device_id=(y * 8 + zh * 2 + h, x * 4 + zl),
+            device_id_type=MESH,
+        )
+
+    def forward_copy(slot):
+        return pltpu.make_async_remote_copy(
+            src_ref=rbuf.at[slot],
+            dst_ref=mrecv.at[slot],
+            send_sem=fw_send.at[slot],
+            recv_sem=mr.at[slot],
+            device_id=(x * 8 + zl * 2 + core, y * 4 + zh),
+            device_id_type=MESH,
+        )
+
+    @pl.when(direct)
+    def _():
+        for h in range(2):
+            mirror_copy(h, core).start()
+
+    for t in range(16):
+
+        @pl.when(XY_PLACE[t] < place_xy)
+        def _():
+            tell(near, xy_mate(t))
+
+    @pl.when(y < x)
+    def _():
+        tell(near, turned)
+
+    for t in range(16):
+
+        @pl.when(Z_LEVEL[t] < rank)
+        def _():
+            for dev in z_mates(t):
+                tell(along, dev)
+
+    wait_some(near, 15 - place_xy + (x < y).astype(jnp.int32))
+
+    @pl.when(relayed)
+    def _():
+        for h in range(2):
+            relay_copy(h, core).start()
 
     for h in range(2):
         here = jnp.logical_and(diag, core == h)
 
-        @pl.when(jnp.logical_not(here))
+        @pl.when(jnp.logical_and(level, jnp.logical_not(here)))
         def _():
             mirror_copy(h, core).start()
 
@@ -202,6 +320,23 @@
     for d in range(16):
         part[1, d, 48:64, :] = jnp.zeros((16, 128), BF16)
 
+    @pl.when(relayed)
+    def _():
+        for slot in range(2):
+            relay_copy(slot, slot).wait_recv()
+
+    wait_some(far, 2 * first.astype(jnp.int32))
+
+    @pl.when(relayed)
+    def _():
+        for slot in range(2):
+            forward_copy(slot).start()
+
+    @pl.when(jnp.logical_and(first, x == y))
+    def _():
+        for h in range(2):
+            mirror_copy(h, core).start()
+
     for h in range(2):
         here = jnp.logical_and(diag, core == h)
 
@@ -314,10 +449,10 @@
     for to in range(16):
         own = jnp.where(core == 0, to // 4, to % 4)
         keep = jnp.where(core == 0, to % 4 // 2, to // 4 // 2)
-        first = pl.multiple_of(8 * own, 8)
+        top = pl.multiple_of(8 * own, 8)
         second = pl.multiple_of(32 + 8 * jnp.where(core == 0, to // 4, to // 4 % 2), 8)
         zbuf[to] = jnp.where(
-            half == keep, red[pl.ds(first, 8), :], pltpu.roll(red[pl.ds(second, 8), :], 64, 1)
+            half == keep, red[pl.ds(top, 8), :], pltpu.roll(red[pl.ds(second, 8), :], 64, 1)
         ).astype(BF16)
 
     def z_copy(k, q):
@@ -340,6 +475,7 @@
             device_id_type=MESH,
         )
 
+    wait_some(along, 2 * (15 - mates))
     z_copies = [z_copy(k, q) for k, q in Z_ORDER]
     for copy in z_copies:
         copy.start()
@@ -352,10 +488,16 @@
         total = total + zrecv[:, k].astype(F32)
     fin_out[...] = total * (1.0 / 512.0)
 
+    @pl.when(relayed)
+    def _():
+        for slot in range(2):
+            relay_copy(slot, core).wait_send()
+            forward_copy(slot).wait_send()
+
     for h in range(2):
         here = jnp.logical_and(diag, core == h)
 
-        @pl.when(jnp.logical_not(here))
+        @pl.when(jnp.logical_not(jnp.logical_or(here, relayed)))
         def _():
             mirror_copy(h, core).wait_send()
 
@@ -439,6 +581,13 @@
             dma((15,)),
             dma((2, 16)),
             dma((2, 16)),
+            vm((2, 128, 128), BF16),
+            dma((2,)),
+            dma((2,)),
+            dma((2,)),
+            pltpu.SemaphoreType.REGULAR,
+            pltpu.SemaphoreType.REGULAR,
+            pltpu.SemaphoreType.REGULAR,
         ],
         compiler_params=pltpu.CompilerParams(
             collective_id=0, has_side_effects=True

time: 48 us -> 45.2 us (0.942)
  Pallas kernels: 47.2 us -> 44.4 us
    pallas_call x1, Pallas kernels: 45.9 us -> 43.1 us  [body(): pl.pallas_call(kernel, out_shape=(pltpu.VMEM((16, 32, 128), BF16), pltpu....]
where the time goes in v3:
time: 45.2 us; the launch traced here: 45 us
  Pallas kernels  44.4 us (98%)
  between operations  0.64 us (1%)
    pallas_call x1, Pallas kernels, body(): pl.pallas_call(kernel, out_shape=(pltpu.VMEM((16, 32, 128), BF16), pltpu....  43.1 us
    pallas_call x1, Pallas kernels, body(): pl.pallas_call(finish, out_shape=(jax.ShapeDtypeStruct((16, 32, 128), BF1...  1.3 us

profile of v3, /device:TPU:1, one launch (start us, length us, event | category | flops | bytes accessed | tf_op | source)
XLA Modules:
  0.0 45.0 jit_solution(11442512180689791576)
XLA Ops:
  0.6 43.1 %shard_map.101 = (bf16[16,32,128]{2,1,0:T(8,128)(2,1)S(1)}, f32[2,8,128]{2,1,0:T(8,128)S(1)}) custom-call(bf16[16,32,128]{2,1,0:T(8,128)(2,1)} %pair_in.1, s32[16,32]{1,0:T(8,128)} %tgt_in.1, bf16[128,512]{1,0:T(8,128)(2,1)} %wg_in.1, bf16[128,512]{1,0:T(8,128)(2,1)} %wu_in.1, bf16[512,128]{1,0:T(8,128)(2,1)} %wo_in.1, bf16[64,128]{1,0:T(8,128)(2,1)} %bitcast.2), custom_call_target="tpu_custom_call" | custom-call | tf_op jit(solution)/shard_map/pallas_call | solution.py:532
  43.7 1.3 %shard_map.102 = (bf16[16,32,128]{2,1,0:T(8,128)(2,1)}, f32[4,32]{1,0:T(4,128)}, f32[4,32]{1,0:T(4,128)}, f32[8,16]{1,0:T(8,128)}, f32[4,4]{1,0:T(4,128)}) custom-call(bf16[16,32,128]{2,1,0:T(8,128)(2,1)S(1)} %get-tuple-element.12.dp_in, f32[2,8,128]{2,1,0:T(8,128)S(1)} %get-tuple-element.13.fin), custom_call_target="tpu_custom_call" | custom-call | tf_op jit(solution)/shard_map/pallas_call | solution.py:596

commit v4 on v3

--- a/solution.py
+++ b/solution.py
@@ -16,6 +16,7 @@
 XY_ORDER = sorted(
     range(1, 16), key=lambda k: -(min(k // 4, 4 - k // 4) + min(k % 4, 4 - k % 4))
 )
+FAR_FIRST = (2, 1, 3, 0)
 Z_ORDER = sorted(
     [(k, q) for k in range(16) for q in range(2) if k + q > 0], key=lambda p: -min(p[0], 16 - p[0])
 )
@@ -82,10 +83,15 @@
     dupb_t,
     dgate,
     dup,
-    part,
-    crecv,
-    xbuf,
-    xrecv,
+    part_a,
+    part_b,
+    crecv_a,
+    crecv_b,
+    xbuf_a,
+    xbuf_b,
+    xrecv_a,
+    xrecv_b,
+    heads,
     red,
     zbuf,
     zrecv,
@@ -317,8 +323,6 @@
     inp_t[...] = jnp.transpose(inp[...])
     upd_t[...] = jnp.transpose(upd[...])
     perm = (lane == (jj % 8) * 16 + prow // 16).astype(BF16)
-    for d in range(16):
-        part[1, d, 48:64, :] = jnp.zeros((16, 128), BF16)
 
     @pl.when(relayed)
     def _():
@@ -355,31 +359,35 @@
         dupd[rows, :] = d_updated
         dupb[rows, :] = d_updated.astype(BF16)
 
-    core_copy = pltpu.make_async_remote_copy(
-        src_ref=part.at[1 - core],
-        dst_ref=crecv,
-        send_sem=cs,
-        recv_sem=cr,
-        device_id=other,
-        device_id_type=MESH,
-    )
-
-    def out_and_head():
+    def core_copy(k, src, dst):
+        return pltpu.make_async_remote_copy(
+            src_ref=src.at[k],
+            dst_ref=dst.at[k],
+            send_sem=cs.at[k],
+            recv_sem=cr.at[k],
+            device_id=other,
+            device_id_type=MESH,
+        )
+
+    def out_and_head(send):
         dupb_t[...] = nt(wdup[...], cot[...]).astype(BF16)
         g_head = nn(upd_t[...], cot[...])
-        g_head = g_head + pltpu.roll(g_head, 64, 1)
-        for a in range(4):
+        heads[...] = g_head + pltpu.roll(g_head, 64, 1)
+        for k in FAR_FIRST:
+            to = lax.rem(x + k, 4)
+            top = pl.multiple_of(to * 32, 32)
             packed = jnp.where(
-                lane[:16] < 64, g_head[32 * a : 32 * a + 16], g_head[32 * a + 16 : 32 * a + 32]
+                lane[:16] < 64, heads[pl.ds(top, 16), :], heads[pl.ds(top + 16, 16), :]
             ).astype(BF16)
+            cols = pl.ds(pl.multiple_of(to * 128, 128), 128)
+            g_out = nn(dupb_t[...], hidden[:, cols]).astype(BF16)
             for b in range(4):
-                part[1, a * 4 + b, 32:48, :] = packed
-        for a in range(4):
-            g_out = nn(dupb_t[...], hidden[:, a * 128 : (a + 1) * 128]).astype(BF16)
-            for b in range(4):
-                part[1, a * 4 + b, 0:32, :] = g_out[32 * b : 32 * b + 32]
-
-    def gate_and_up():
+                part_b[k, b, 0:32, :] = g_out[32 * b : 32 * b + 32]
+                part_b[k, b, 32:48, :] = packed
+            if send:
+                core_copy(k, part_b, crecv_b).start()
+
+    def gate_and_up(send):
         for h in range(2):
             rows = pl.ds(h * 256, 256)
             for n in range(2):
@@ -387,45 +395,59 @@
                 d_hidden = nn(dupb[rows, :], wo_t[:, cols])
                 dgate[rows, cols] = (d_hidden * slope[rows, cols]).astype(BF16)
                 dup[rows, cols] = (d_hidden * swish[rows, cols]).astype(BF16)
-        for b in range(4):
-            cols = slice(b * 128, (b + 1) * 128)
+        for k in FAR_FIRST:
+            cols = pl.ds(pl.multiple_of(lax.rem(y + k, 4) * 128, 128), 128)
             g_gate = nn(inp_t[...], dgate[:, cols]).astype(BF16)
             g_up = nn(inp_t[...], dup[:, cols]).astype(BF16)
             for a in range(4):
-                part[0, a * 4 + b, 0:32, :] = g_gate[32 * a : 32 * a + 32]
-                part[0, a * 4 + b, 32:64, :] = g_up[32 * a : 32 * a + 32]
-
-    @pl.when(core == 0)
-    def _():
-        out_and_head()
-        core_copy.start()
-        gate_and_up()
-
-    @pl.when(core == 1)
-    def _():
-        gate_and_up()
-        core_copy.start()
-        out_and_head()
-
-    core_copy.wait_recv()
-    for d in range(16):
-        xbuf[d] = (part[core, d].astype(F32) + crecv[d].astype(F32)).astype(BF16)
-
-    def xy_copy(k):
-        dev = xy_dev(k)
-        to = (x + k // 4) % 4 * 4 + (y + k % 4) % 4
+                part_a[k, a, 0:32, :] = g_gate[32 * a : 32 * a + 32]
+                part_a[k, a, 32:64, :] = g_up[32 * a : 32 * a + 32]
+            if send:
+                core_copy(k, part_a, crecv_a).start()
+
+    def xy_copy(k, src, dst):
+        dx, dy = k // 4, k % 4
+        if src is xbuf_a:
+            piece = src.at[dy, lax.rem(x + dx, 4)]
+        else:
+            piece = src.at[dx, lax.rem(y + dy, 4)]
         return pltpu.make_async_remote_copy(
-            src_ref=xbuf.at[to],
-            dst_ref=xrecv.at[k - 1],
+            src_ref=piece,
+            dst_ref=dst.at[k - 1],
             send_sem=xs.at[k - 1],
             recv_sem=xr.at[k - 1],
-            device_id=dev,
+            device_id=xy_dev(k),
             device_id_type=MESH,
         )
 
-    xy_copies = {k: xy_copy(k) for k in XY_ORDER}
-    for k in XY_ORDER:
-        xy_copies[k].start()
+    def spread_plane(part, crecv, xbuf, xrecv):
+        for k in FAR_FIRST:
+            core_copy(k, part, crecv).wait_recv()
+            for n in range(4):
+                xbuf[k, n] = (part[k, n].astype(F32) + crecv[k, n].astype(F32)).astype(BF16)
+            for n in FAR_FIRST:
+                step = n * 4 + k if xbuf is xbuf_a else k * 4 + n
+                if step > 0:
+                    xy_copy(step, xbuf, xrecv).start()
+
+    def gather_plane(own, xbuf, xrecv):
+        total = own.astype(F32)
+        for k in reversed(XY_ORDER):
+            xy_copy(k, xbuf, xrecv).wait_recv()
+            total = total + xrecv[k - 1].astype(F32)
+        return total
+
+    @pl.when(core == 0)
+    def _():
+        out_and_head(True)
+        gate_and_up(False)
+        spread_plane(part_a, crecv_a, xbuf_a, xrecv_a)
+
+    @pl.when(core == 1)
+    def _():
+        gate_and_up(True)
+        out_and_head(False)
+        spread_plane(part_b, crecv_b, xbuf_b, xrecv_b)
 
     for h in range(2):
         rows = pl.ds(h * 256, 256)
@@ -440,11 +462,14 @@
             (dupd[rows, :] + d_norm).astype(BF16).reshape(16, 16, 128)
         )
 
-    total = xbuf[x * 4 + y].astype(F32)
-    for k in reversed(XY_ORDER):
-        xy_copies[k].wait_recv()
-        total = total + xrecv[k - 1].astype(F32)
-    red[...] = total
+    @pl.when(core == 0)
+    def _():
+        red[...] = gather_plane(xbuf_a[0, x], xbuf_a, xrecv_a)
+
+    @pl.when(core == 1)
+    def _():
+        red[0:48, :] = gather_plane(xbuf_b[0, y], xbuf_b, xrecv_b)
+
     half = lane[:8] // 64
     for to in range(16):
         own = jnp.where(core == 0, to // 4, to % 4)
@@ -501,27 +526,50 @@
         def _():
             mirror_copy(h, core).wait_send()
 
-    core_copy.wait_send()
-    for k in XY_ORDER:
-        xy_copies[k].wait_send()
+    @pl.when(core == 0)
+    def _():
+        for k in range(4):
+            core_copy(k, part_b, crecv_b).wait_send()
+        for k in XY_ORDER:
+            xy_copy(k, xbuf_a, xrecv_a).wait_send()
+
+    @pl.when(core == 1)
+    def _():
+        for k in range(4):
+            core_copy(k, part_a, crecv_a).wait_send()
+        for k in XY_ORDER:
+            xy_copy(k, xbuf_b, xrecv_b).wait_send()
+
     for copy in z_copies:
         copy.wait_send()
 
 
-def finish(dp_in, fin, dp_out, gg_out, gu_out, go_out, gh_out, sem):
-    store = pltpu.make_async_copy(dp_in, dp_out, sem)
-    store.start()
+def finish(
+    dp_in, fin, dp_out, gg_out, gu_out, go_out, gh_out, gg, gu, go, gh, sem
+):
+    stores = [
+        pltpu.make_async_copy(src, dst, sem.at[n])
+        for n, (src, dst) in enumerate(
+            ((dp_in, dp_out), (gg, gg_out), (gu, gu_out), (go, go_out), (gh, gh_out))
+        )
+    ]
+    stores[0].start()
     r = lax.axis_index("row")
     c = lax.axis_index("col")
-    zh, core, y, zl = (r // 2) % 4, r % 2, c // 4, c % 4
-    a_tile = pltpu.roll(fin[0], (128 - 32 * zl) % 128, 1)
-    gg_out[...] = jnp.where(core == 0, a_tile[0:4, 0:32], a_tile[4:8, 0:32])
-    gu_out[...] = jnp.where(core == 0, a_tile[0:4, 64:96], a_tile[4:8, 64:96])
+    chip, core = lax.div(r, 2), lax.rem(r, 2)
+    zh, y, zl = lax.rem(chip, 4), lax.div(c, 4), lax.rem(c, 4)
+    a_tile = pltpu.roll(fin[0], lax.rem(128 - 32 * zl, 128), 1)
+    gg[...] = jnp.where(core == 0, a_tile[0:4, 0:32], a_tile[4:8, 0:32])
+    gu[...] = jnp.where(core == 0, a_tile[0:4, 64:96], a_tile[4:8, 64:96])
     b_tile = fin[1]
-    go_out[...] = pltpu.roll(b_tile, (128 - (32 * zh + 16 * core)) % 128, 1)[:, :16]
-    h_tile = pltpu.roll(b_tile, (192 - (64 * (zh // 2) + 16 * y + 4 * zl)) % 128, 1)
-    gh_out[...] = jnp.where(core == 0, h_tile[0:4, :4], h_tile[4:8, :4])
-    store.wait()
+    go[...] = pltpu.roll(b_tile, lax.rem(128 - (32 * zh + 16 * core), 128), 1)[:, :16]
+    at = 64 * lax.div(zh, 2) + 16 * y + 4 * zl
+    h_tile = pltpu.roll(b_tile, lax.rem(192 - at, 128), 1)
+    gh[...] = jnp.where(core == 0, h_tile[0:4, :4], h_tile[4:8, :4])
+    for store in stores[1:]:
+        store.start()
+    for store in stores:
+        store.wait()
 
 
 def body(pair, targets, w_gate, w_up, w_out, w_head):
@@ -565,18 +613,23 @@
             vm((128, 512), BF16),
             vm((512, 512), BF16),
             vm((512, 512), BF16),
-            vm((2, 16, 64, 128), BF16),
-            vm((16, 64, 128), BF16),
-            vm((16, 64, 128), BF16),
+            vm((4, 4, 64, 128), BF16),
+            vm((4, 4, 48, 128), BF16),
+            vm((4, 4, 64, 128), BF16),
+            vm((4, 4, 48, 128), BF16),
+            vm((4, 4, 64, 128), BF16),
+            vm((4, 4, 48, 128), BF16),
             vm((15, 64, 128), BF16),
+            vm((15, 48, 128), BF16),
+            vm((128, 128), F32),
             vm((64, 128), F32),
             vm((16, 8, 128), BF16),
             vm((2, 16, 8, 128), BF16),
             dma((6,)),
             dma((2,)),
             dma((2,)),
-            dma,
-            dma,
+            dma((4,)),
+            dma((4,)),
             dma((15,)),
             dma((15,)),
             dma((2, 16)),
@@ -603,8 +656,8 @@
             jax.ShapeDtypeStruct((4, 4), F32),
         ),
         in_specs=[vmem, vmem],
-        out_specs=(anywhere, vmem, vmem, vmem, vmem),
-        scratch_shapes=[dma],
+        out_specs=(anywhere,) * 5,
+        scratch_shapes=[vm((4, 32), F32), vm((4, 32), F32), vm((8, 16), F32), vm((4, 4), F32), dma((5,))],
         compiler_params=pltpu.CompilerParams(vmem_limit_bytes=16 * 2**20),
     )(d_pair, fin)
     return d_pair, g_gate, g_up, g_out.T, g_head

time: 45.2 us -> 44.5 us (0.985)
  Pallas kernels: 44.4 us -> 43.7 us
    pallas_call x1, Pallas kernels: 1.3 us -> 0.79 us  [body(): pl.pallas_call(finish, out_shape=(jax.ShapeDtypeStruct((16, 32, 128), BF1...]
where the time goes in v4:
time: 44.5 us; the launch traced here: 44.4 us
  Pallas kernels  43.7 us (98%)
  between operations  0.64 us (1%)
    pallas_call x1, Pallas kernels, body(): pl.pallas_call(kernel, out_shape=(pltpu.VMEM((16, 32, 128), BF16), pltpu....  42.9 us

profile of v4, /device:TPU:1, one launch (start us, length us, event | category | flops | bytes accessed | tf_op | source)
XLA Modules:
  0.0 44.4 jit_solution(9874538422303564315)
XLA Ops:
  0.6 42.9 %shard_map.101 = (bf16[16,32,128]{2,1,0:T(8,128)(2,1)S(1)}, f32[2,8,128]{2,1,0:T(8,128)S(1)}) custom-call(bf16[16,32,128]{2,1,0:T(8,128)(2,1)} %pair_in.1, s32[16,32]{1,0:T(8,128)} %tgt_in.1, bf16[128,512]{1,0:T(8,128)(2,1)} %wg_in.1, bf16[128,512]{1,0:T(8,128)(2,1)} %wu_in.1, bf16[512,128]{1,0:T(8,128)(2,1)} %wo_in.1, bf16[64,128]{1,0:T(8,128)(2,1)} %bitcast.2), custom_call_target="tpu_custom_call" | custom-call | tf_op jit(solution)/shard_map/pallas_call | solution.py:580
  43.6 0.8 %shard_map.102 = (bf16[16,32,128]{2,1,0:T(8,128)(2,1)}, f32[4,32]{1,0:T(4,128)}, f32[4,32]{1,0:T(4,128)}, f32[8,16]{1,0:T(8,128)}, f32[4,4]{1,0:T(4,128)}) custom-call(bf16[16,32,128]{2,1,0:T(8,128)(2,1)S(1)} %get-tuple-element.12.dp_in, f32[2,8,128]{2,1,0:T(8,128)S(1)} %get-tuple-element.13.fin), custom_call_target="tpu_custom_call" | custom-call | tf_op jit(solution)/shard_map/pallas_call | solution.py:649

commit v5 on v4

--- a/solution.py
+++ b/solution.py
@@ -359,6 +359,8 @@
         dupd[rows, :] = d_updated
         dupb[rows, :] = d_updated.astype(BF16)
 
+    lead = 1 - core
+
     def core_copy(k, src, dst):
         return pltpu.make_async_remote_copy(
             src_ref=src.at[k],
@@ -437,13 +439,13 @@
             total = total + xrecv[k - 1].astype(F32)
         return total
 
-    @pl.when(core == 0)
+    @pl.when(lead == 0)
     def _():
         out_and_head(True)
         gate_and_up(False)
         spread_plane(part_a, crecv_a, xbuf_a, xrecv_a)
 
-    @pl.when(core == 1)
+    @pl.when(lead == 1)
     def _():
         gate_and_up(True)
         out_and_head(False)
@@ -462,20 +464,20 @@
             (dupd[rows, :] + d_norm).astype(BF16).reshape(16, 16, 128)
         )
 
-    @pl.when(core == 0)
+    @pl.when(lead == 0)
     def _():
         red[...] = gather_plane(xbuf_a[0, x], xbuf_a, xrecv_a)
 
-    @pl.when(core == 1)
+    @pl.when(lead == 1)
     def _():
         red[0:48, :] = gather_plane(xbuf_b[0, y], xbuf_b, xrecv_b)
 
     half = lane[:8] // 64
     for to in range(16):
-        own = jnp.where(core == 0, to // 4, to % 4)
-        keep = jnp.where(core == 0, to % 4 // 2, to // 4 // 2)
+        own = jnp.where(lead == 0, to // 4, to % 4)
+        keep = jnp.where(lead == 0, to % 4 // 2, to // 4 // 2)
         top = pl.multiple_of(8 * own, 8)
-        second = pl.multiple_of(32 + 8 * jnp.where(core == 0, to // 4, to // 4 % 2), 8)
+        second = pl.multiple_of(32 + 8 * jnp.where(lead == 0, to // 4, to // 4 % 2), 8)
         zbuf[to] = jnp.where(
             half == keep, red[pl.ds(top, 8), :], pltpu.roll(red[pl.ds(second, 8), :], 64, 1)
         ).astype(BF16)
@@ -483,9 +485,9 @@
     def z_copy(k, q):
         return pltpu.make_async_remote_copy(
             src_ref=zbuf.at[(z + k) % 16],
-            dst_ref=zrecv.at[core, k],
+            dst_ref=zrecv.at[lead, k],
             send_sem=zs.at[q, k],
-            recv_sem=zr.at[core, k],
+            recv_sem=zr.at[lead, k],
             device_id=z_dev(k, q),
             device_id_type=MESH,
         )
@@ -504,8 +506,8 @@
     z_copies = [z_copy(k, q) for k, q in Z_ORDER]
     for copy in z_copies:
         copy.start()
-    zrecv[core, 0] = zbuf[z]
-    z_arrival(0, 1 - core).wait_recv()
+    zrecv[lead, 0] = zbuf[z]
+    z_arrival(0, core).wait_recv()
     total = zrecv[:, 0].astype(F32)
     for k in sorted(range(1, 16), key=lambda k: min(k, 16 - k)):
         z_arrival(k, 0).wait_recv()
@@ -526,14 +528,14 @@
         def _():
             mirror_copy(h, core).wait_send()
 
-    @pl.when(core == 0)
+    @pl.when(lead == 0)
     def _():
         for k in range(4):
             core_copy(k, part_b, crecv_b).wait_send()
         for k in XY_ORDER:
             xy_copy(k, xbuf_a, xrecv_a).wait_send()
 
-    @pl.when(core == 1)
+    @pl.when(lead == 1)
     def _():
         for k in range(4):
             core_copy(k, part_a, crecv_a).wait_send()

time: 44.5 us -> 44.4 us (level)
  no operation moved by 1% of the time
where the time goes in v5:
time: 44.4 us; the launch traced here: 44.3 us
  Pallas kernels  43.7 us (98%)
  between operations  0.64 us (1%)
    pallas_call x1, Pallas kernels, body(): pl.pallas_call(kernel, out_shape=(pltpu.VMEM((16, 32, 128), BF16), pltpu....  42.9 us

profile of v5, /device:TPU:1, one launch (start us, length us, event | category | flops | bytes accessed | tf_op | source)
XLA Modules:
  0.0 44.3 jit_solution(5843394045686525843)
XLA Ops:
  0.6 42.9 %shard_map.101 = (bf16[16,32,128]{2,1,0:T(8,128)(2,1)S(1)}, f32[2,8,128]{2,1,0:T(8,128)S(1)}) custom-call(bf16[16,32,128]{2,1,0:T(8,128)(2,1)} %pair_in.1, s32[16,32]{1,0:T(8,128)} %tgt_in.1, bf16[128,512]{1,0:T(8,128)(2,1)} %wg_in.1, bf16[128,512]{1,0:T(8,128)(2,1)} %wu_in.1, bf16[512,128]{1,0:T(8,128)(2,1)} %wo_in.1, bf16[64,128]{1,0:T(8,128)(2,1)} %bitcast.2), custom_call_target="tpu_custom_call" | custom-call | tf_op jit(solution)/shard_map/pallas_call | solution.py:582
  43.5 0.8 %shard_map.102 = (bf16[16,32,128]{2,1,0:T(8,128)(2,1)}, f32[4,32]{1,0:T(4,128)}, f32[4,32]{1,0:T(4,128)}, f32[8,16]{1,0:T(8,128)}, f32[4,4]{1,0:T(4,128)}) custom-call(bf16[16,32,128]{2,1,0:T(8,128)(2,1)S(1)} %get-tuple-element.12.dp_in, f32[2,8,128]{2,1,0:T(8,128)S(1)} %get-tuple-element.13.fin), custom_call_target="tpu_custom_call" | custom-call | tf_op jit(solution)/shard_map/pallas_call | solution.py:651
